TPU v7x, 128 devices: a whole 4x4x4 slice. The times are simulated.
128 devices in a mesh: dp: 4 (over x_hi, core), patch: 32 (over y, x_lo, z).
Axes of the slice: x: 4 (x_hi: 2, x_lo: 2; x = x_hi * 2 + x_lo), y: 4, z: 4, core: 2. Of those that a mesh axis runs over, the one named last changes fastest.
Arguments:
- query_tokens: bfloat16 [4, 64, 128, 768], P('dp', 'patch')
- past_tokens: bfloat16 [4, 256, 128, 768], P('dp', 'patch'), may hold values from -6 to 6
- source_dev: int32 [64, 4, 3], replicated, may hold values from 0 to 31, all different within a row; in each aligned block of 8 rows (0 to 7, 8 to 15, ..., all dimensions but the last counted through in order) at most 2 rows name the same one
- source_slot: int32 [64, 4, 3], replicated, may hold values from 0 to 7
- kept: int32 [64, 4, 3], replicated, may hold values 0 or 1
- w_query: bfloat16 [768, 768], replicated
- w_key: bfloat16 [768, 768], replicated
- w_value: bfloat16 [768, 768], replicated, may hold values from -0.21875 to 0.21875
- w_out: bfloat16 [768, 768], replicated, may hold values from -0.875 to 0.875
- grad_out: bfloat16 [4, 64, 128, 768], P('dp', 'patch'), may hold values from -6 to 6
Outputs:
- attn_out: bfloat16 [4, 64, 128, 768], P('dp', 'patch')
- grad_query_tokens: bfloat16 [4, 64, 128, 768], P('dp', 'patch')
- grad_past_tokens: bfloat16 [4, 256, 128, 768], P('dp', 'patch')
- grad_w_query: float32 [768, 768], replicated
- grad_w_key: float32 [768, 768], replicated
- grad_w_value: float32 [768, 768], replicated
- grad_w_out: float32 [768, 768], replicated
Inputs may be any that keep to these rules, and one draw needn't show every extreme that they name: `source_dev`: row (p, f) lists the devices holding the frame-f blocks that patch p reads: 3 different devices a row. Over the rows of one device's 2 patches, no device is listed more than 2 times, and some device is listed exactly 2 times.
All inputs are finite; a program needn't handle non-finite values.
Results may differ from a plain program's by a relative error of at most 0.013.
The roundings to bfloat16 on the way count: a program that leaves them out, or rounds other values in their place, can miss the bound.
Values may be sent and summed in bfloat16 or wider, within the bound.
A program may use at most 256 MiB of HBM per device.

v0:
```python
import math

import jax
import jax.numpy as jnp
from jax import lax
from jax.experimental import pallas as pl
from jax.experimental.pallas import tpu as pltpu
from jax.sharding import PartitionSpec as P

H = 12
HD = 64
F32 = jnp.float32
MESH = pl.DeviceIdType.MESH
BF16 = jnp.bfloat16
NN = (((1,), (0,)), ((), ()))
NT = (((1,), (1,)), ((), ()))
TN = (((0,), (0,)), ((), ()))


def mm(a, b, dims=NN):
    return lax.dot_general(a, b, dims, preferred_element_type=F32)


def place():
    device = lax.axis_index("patch")
    return device // 8, (device // 4) % 2, device % 4, lax.axis_index("dp")


def step_id(y, x, z, dim, hop):
    return ((y + hop * (1 - dim)) % 4) * 8 + x * 4 + (z + hop * dim) % 4


def meet(y, x, z, dp, across):
    barrier = pltpu.get_barrier_semaphore()
    ids = [step_id(y, x, z, dim, hop) for dim in (0, 1) for hop in (1, 2, 3)]
    if across:
        ids.append(y * 8 + (1 - x) * 4 + z)
    for other in ids:
        pl.semaphore_signal(barrier, 1, device_id=(dp, other), device_id_type=MESH)
    pl.semaphore_wait(barrier, len(ids))


def spread(past, table, cap, ident):
    blocks, rows, width = past.shape
    parts = 4
    chunk = blocks // parts

    def kernel(
        table_ref, past_ref, out_ref, have_a, have_b, sel_a, sel_b,
        in_sem, x_send, x_recv, g_send, g_recv, e_send, e_recv, own_sem,
    ):
        y, x, z, dp = place()
        pos = lambda dim, hop=0: (y * (1 - dim) + z * dim + hop) % 4
        have, sel = (have_a, have_b), (sel_a, sel_b)
        half = (x, 1 - x)

        def region(t, hop, c):
            return have[t].at[pl.ds(pos(half[t], hop) * blocks + c * chunk, chunk)]

        local = pltpu.make_async_copy(
            past_ref, have_a.at[pl.ds(pos(half[0]) * blocks, blocks)], in_sem
        )
        local.start()
        meet(y, x, z, dp, True)

        def cross(c):
            at = pl.ds(pos(half[0]) * blocks + c * chunk, chunk)
            return pltpu.make_async_remote_copy(
                past_ref.at[pl.ds(c * chunk, chunk)], have_b.at[at], x_send.at[c], x_recv.at[c],
                device_id=(dp, y * 8 + (1 - x) * 4 + z), device_id_type=MESH,
            )

        def crossed(c):
            at = pl.ds(pos(half[1]) * blocks + c * chunk, chunk)
            return pltpu.make_async_remote_copy(
                past_ref.at[pl.ds(c * chunk, chunk)], have_b.at[at], x_send.at[c], x_recv.at[c],
                device_id=(dp, y * 8 + (1 - x) * 4 + z), device_id_type=MESH,
            )

        turn = (0, 2, 1, 3)
        ways = [(way, 0, c) for c in turn for way in ((1, 3) if c < 2 else (3, 1))]
        ways += [(1, 3, c) if c < 2 else (3, 1, c) for c in turn]

        def go(t, n):
            way, owner, c = ways[n]
            return pltpu.make_async_remote_copy(
                region(t, owner, c), region(t, owner, c), g_send.at[t, n], g_recv.at[t, n],
                device_id=(dp, step_id(y, x, z, half[t], way)), device_id_type=MESH,
            )

        def came(t, n):
            way, owner, c = ways[n]
            owner = (owner - way) % 4
            return pltpu.make_async_remote_copy(
                region(t, owner, c), region(t, owner, c), g_send.at[t, n], g_recv.at[t, n],
                device_id=(dp, step_id(y, x, z, half[t], way)), device_id_type=MESH,
            )

        def swap(t, hop, arriving=False):
            h = half[t]
            at = h * 4 + pos(1 - h, -hop if arriving else 0)
            return pltpu.make_async_remote_copy(
                sel[t].at[hop], out_ref.at[pl.ds(at * cap, cap)],
                e_send.at[t, hop - 1], e_recv.at[t, hop - 1],
                device_id=(dp, step_id(y, x, z, 1 - h, hop)), device_id_type=MESH,
            )

        def keep(t):
            h = half[t]
            at = h * 4 + pos(1 - h)
            return pltpu.make_async_copy(
                sel[t].at[0], out_ref.at[pl.ds(at * cap, cap)], own_sem.at[t]
            )

        def choose(t):
            h = half[t]
            for hop in (2, 1, 3, 0):
                row = h * 4 + pos(1 - h, hop)

                @pl.loop(0, cap)
                def _(s):
                    sel[t][hop, s] = have[t][table_ref[row * cap + s]]

                if hop:
                    swap(t, hop).start()
                else:
                    keep(t).start()

        for c in turn:
            cross(c).start()
        local.wait()
        for n in range(2 * parts):
            go(0, n).start()

        def relay(t, i):
            came(t, 2 * i).wait_recv()
            go(t, 2 * parts + i).start()

        for i in range(parts):
            crossed(turn[i]).wait_recv()
            go(1, 2 * i).start()
            go(1, 2 * i + 1).start()
            relay(0, i)
        for i in range(parts):
            relay(1, i)
        for t in (0, 1):
            for n in range(2 * parts):
                if n % 2:
                    came(t, n).wait_recv()
            for n in range(2 * parts, 3 * parts):
                came(t, n).wait_recv()
        choose(0)
        choose(1)
        for t in (0, 1):
            for hop in (1, 2, 3):
                swap(t, hop, True).wait_recv()
            keep(t).wait()
        for c in turn:
            cross(c).wait_send()
        for t in (0, 1):
            for n in range(3 * parts):
                go(t, n).wait_send()
            for hop in (1, 2, 3):
                swap(t, hop).wait_send()

    return pl.pallas_call(
        kernel,
        out_shape=jax.ShapeDtypeStruct((table.shape[0], rows, width), past.dtype),
        in_specs=[pl.BlockSpec(memory_space=pltpu.SMEM), pl.BlockSpec(memory_space=pl.ANY)],
        out_specs=pl.BlockSpec(memory_space=pl.ANY),
        scratch_shapes=[
            pltpu.VMEM((4 * blocks, rows, width), past.dtype),
            pltpu.VMEM((4 * blocks, rows, width), past.dtype),
            pltpu.VMEM((4, cap, rows, width), past.dtype),
            pltpu.VMEM((4, cap, rows, width), past.dtype),
            pltpu.SemaphoreType.DMA,
            pltpu.SemaphoreType.DMA((parts,)),
            pltpu.SemaphoreType.DMA((parts,)),
            pltpu.SemaphoreType.DMA((2, 3 * parts)),
            pltpu.SemaphoreType.DMA((2, 3 * parts)),
            pltpu.SemaphoreType.DMA((2, 3)),
            pltpu.SemaphoreType.DMA((2, 3)),
            pltpu.SemaphoreType.DMA((2,)),
        ],
        compiler_params=pltpu.CompilerParams(
            collective_id=ident, has_side_effects=True, vmem_limit_bytes=48 << 20
        ),
        name="spread",
    )(table, past)


def send_back(grads, tokens, grad_out, seen, dkv, dq, mixed, cap, ident):
    _, rows, width = grads.shape
    total = seen.shape[0]
    chunk = total // 8

    def kernel(
        grad_ref, tok_in, gout_in, seen_in, dkv_in, dq_in, mixed_in,
        out_ref, wq_ref, wk_ref, wv_ref, wo_ref, own, send, recv, own_sem,
        tok_ref, gout_ref, seen_ref, dkv_ref, dq_ref, mixed_ref, op_sem,
    ):
        pairs = (
            (tok_in, tok_ref), (dq_in, dq_ref), (mixed_in, mixed_ref), (gout_in, gout_ref),
            (seen_in, seen_ref), (dkv_in, dkv_ref),
        )
        operands = [pltpu.make_async_copy(a, b, op_sem.at[i]) for i, (a, b) in enumerate(pairs)]
        y, x, z, dp = place()
        pos = lambda dim, hop=0: (y * (1 - dim) + z * dim + hop) % 4
        part = lambda ref, at: ref.at[pl.ds(at * cap, cap)]

        def swap(h, hop, arriving=False):
            return pltpu.make_async_remote_copy(
                part(grad_ref, h * 4 + pos(1 - h, hop)),
                part(out_ref, h * 4 + pos(1 - h, -hop if arriving else 0)),
                send.at[h, hop - 1], recv.at[h, hop - 1],
                device_id=(dp, step_id(y, x, z, 1 - h, hop)), device_id_type=MESH,
            )

        def load(h):
            return pltpu.make_async_copy(
                part(grad_ref, h * 4 + pos(1 - h)), own.at[h], own_sem.at[h]
            )

        def store(h):
            return pltpu.make_async_copy(
                own.at[h], part(out_ref, h * 4 + pos(1 - h)), own_sem.at[h]
            )

        for h in (0, 1):
            load(h).start()
        meet(y, x, z, dp, False)
        for hop in (2, 1, 3):
            for h in (0, 1):
                swap(h, hop).start()
        for h in (0, 1):
            load(h).wait()
            store(h).start()
        for operand in operands:
            operand.start()
        for operand in operands:
            operand.wait()
        wq_ref[...] = mm(tok_ref[...], dq_ref[...], TN)
        wo_ref[...] = mm(mixed_ref[...], gout_ref[...], TN)
        wk_ref[...] = jnp.zeros_like(wk_ref)
        wv_ref[...] = jnp.zeros_like(wv_ref)

        @pl.loop(0, total // chunk)
        def _(n):
            at = pl.ds(pl.multiple_of(n * chunk, 16), chunk)
            left = seen_ref[at]
            wk_ref[...] += mm(left, dkv_ref[at, :width], TN)
            wv_ref[...] += mm(left, dkv_ref[at, width:], TN)

        for h in (0, 1):
            store(h).wait()
            for hop in (1, 2, 3):
                swap(h, hop, True).wait_recv()
        for h in (0, 1):
            for hop in (1, 2, 3):
                swap(h, hop).wait_send()

    return pl.pallas_call(
        kernel,
        out_shape=(jax.ShapeDtypeStruct(grads.shape, grads.dtype),)
        + (jax.ShapeDtypeStruct((width, width), F32),) * 4,
        in_specs=[pl.BlockSpec(memory_space=pl.ANY)] * 7,
        out_specs=(pl.BlockSpec(memory_space=pl.ANY),) + (pl.BlockSpec(memory_space=pltpu.VMEM),) * 4,
        scratch_shapes=[
            pltpu.VMEM((2, cap, rows, width), grads.dtype),
            pltpu.SemaphoreType.DMA((2, 3)),
            pltpu.SemaphoreType.DMA((2, 3)),
            pltpu.SemaphoreType.DMA((2,)),
        ]
        + [pltpu.VMEM(a.shape, a.dtype) for a in (tokens, grad_out, seen, dkv, dq, mixed)]
        + [pltpu.SemaphoreType.DMA((6,))],
        compiler_params=pltpu.CompilerParams(
            collective_id=ident, has_side_effects=True, vmem_limit_bytes=56 << 20
        ),
        name="send_back",
    )(grads, tokens, grad_out, seen, dkv, dq, mixed)


def collect(partial, grads, scale):
    groups, blocks, rows, width = partial.shape
    chunk = blocks // 4
    w_rows = grads[0].shape[0]
    block = w_rows // 24
    half_w = 48

    def collect_steps(
        part_in, part_ref, part_sem, out_ref, relay, staged, inward, mine, across,
        r_send, r_recv, d_send, d_recv, x_send, x_recv,
    ):
        y, x, z, dp = place()
        pos = lambda dim, hop=0: (y * (1 - dim) + z * dim + hop) % 4
        half = (1 - x, x)
        held = pltpu.make_async_copy(part_in, part_ref, part_sem)
        held.start()
        ways = (3, 1)
        side_of = (0, 0, 1, 1)

        def row(t, hop):
            return half[t] * 4 + pos(half[t], hop)

        def span(c):
            return pl.ds(c * chunk, chunk)

        def send_to(source, target, sends, recvs, t, side):
            return pltpu.make_async_remote_copy(
                source, target, sends, recvs,
                device_id=(dp, step_id(y, x, z, half[t], ways[side])), device_id_type=MESH,
            )

        def pass_on(t, c):
            return send_to(
                part_in.at[row(t, 2), span(c)], relay.at[t, span(c)],
                r_send.at[t, c], r_recv.at[t, c], t, side_of[c],
            )

        def plain(t, c):
            side = 1 - side_of[c]
            return send_to(
                part_in.at[row(t, ways[side]), span(c)], inward.at[t, side, span(c)],
                d_send.at[t, c, 0], d_recv.at[t, c, 0], t, side,
            )

        def summed(t, c):
            side = side_of[c]
            return send_to(
                staged.at[t, span(c)], inward.at[t, side, span(c)],
                d_send.at[t, c, 1], d_recv.at[t, c, 1], t, side,
            )

        def cross(c):
            return pltpu.make_async_remote_copy(
                mine.at[span(c)], across.at[span(c)], x_send.at[c], x_recv.at[c],
                device_id=(dp, y * 8 + (1 - x) * 4 + z), device_id_type=MESH,
            )

        def final(t, b):
            return (
                part_ref[row(t, 0), b].astype(F32)
                + inward[t, 0, b].astype(F32)
                + inward[t, 1, b].astype(F32)
            )

        def join(t, c):
            pass_on(t, c).wait_recv()

            @pl.loop(c * chunk, c * chunk + chunk)
            def _(b):
                own = part_ref[row(t, ways[side_of[c]]), b]
                staged[t, b] = (own.astype(F32) + relay[t, b].astype(F32)).astype(staged.dtype)

            summed(t, c).start()

        def arrive(t, c):
            plain(t, c).wait_recv()
            summed(t, c).wait_recv()

        def finish_other(c):
            arrive(0, c)

            @pl.loop(c * chunk, c * chunk + chunk)
            def _(b):
                mine[b] = final(0, b).astype(mine.dtype)

            cross(c).start()

        for c in (0, 2, 1, 3):
            for t in (0, 1):
                pass_on(t, c).start()
        for c in (2, 0):
            for t in (0, 1):
                plain(t, c).start()
        yield
        held.wait()
        for c in (0, 2):
            for t in (0, 1):
                join(t, c)
                plain(t, 3 - c).start()
        yield
        for c in (1, 3):
            for t in (0, 1):
                join(t, c)
        yield
        for c in (0, 2):
            finish_other(c)
        yield
        for c in (1, 3):
            finish_other(c)
        yield
        for c in (0, 2, 1, 3):
            arrive(1, c)
            cross(c).wait_recv()

            @pl.loop(c * chunk, c * chunk + chunk)
            def _(b):
                out_ref[b] = (final(1, b) + across[b].astype(F32)).astype(out_ref.dtype)

        yield
        for c in range(4):
            cross(c).wait_send()
            for t in (0, 1):
                pass_on(t, c).wait_send()
                plain(t, c).wait_send()
                summed(t, c).wait_send()

    def reduce_steps(
        given, refs, grad_sem, out_ref, acc, stage, peer, mid, in_a, mid_b, in_b, in_c, got_b, full,
        core_send, core_recv, send, recv, back_send, back_recv, out_sem,
    ):
        y, x_low, z, dp = place()
        core = dp % 2
        spot = {"x": (dp // 2) * 2 + x_low, "y": y, "z": z}
        orders = ("xyz", "yzx", "zxy")
        a_ref, b_ref, c_ref, d_ref = refs
        loads = [pltpu.make_async_copy(given[i], refs[i], grad_sem.at[i]) for i in range(4)]
        for load in loads:
            load.start()

        def there(axis, hop):
            at = dict(spot)
            at[axis] = (at[axis] + hop) % 4
            return (
                (at["x"] // 2) * 2 + core,
                at["y"] * 8 + (at["x"] % 2) * 4 + at["z"],
            )

        other = (dp + 1 - 2 * core, y * 8 + x_low * 4 + z)
        barrier = pltpu.get_barrier_semaphore()
        for axis in "xyz":
            for hop in (1, 2, 3):
                pl.semaphore_signal(barrier, 1, device_id=there(axis, hop), device_id_type=MESH)
        pl.semaphore_signal(barrier, 1, device_id=other, device_id_type=MESH)
        pl.semaphore_wait(barrier, 10)
        yield
        for load in loads:
            load.wait()

        def take(keep, give):
            for i in (0, 1):
                @pl.loop(0, half_w // 2)
                def _(n):
                    at = pl.ds(pl.multiple_of(n * block, block), block)
                    stage[i * (half_w // 2) + n] = (give[i][at] * scale).astype(BF16)
                    acc[i * (half_w // 2) + n] = keep[i][at] * scale

        @pl.when(core == 0)
        def _():
            take((a_ref, b_ref), (c_ref, d_ref))

        @pl.when(core == 1)
        def _():
            take((c_ref, d_ref), (a_ref, b_ref))

        def pair(p):
            at = pl.ds(p * 16, 16)
            return pltpu.make_async_remote_copy(
                stage.at[at], peer.at[at], core_send.at[p], core_recv.at[p],
                device_id=other, device_id_type=MESH,
            )

        def copy(source, target, phase, p, hop, sems=None):
            s, r = sems or (send, recv)
            return pltpu.make_async_remote_copy(
                source, target, s.at[phase, p, hop - 1], r.at[phase, p, hop - 1],
                device_id=there(orders[p][(0, 1, 2, 1, 0)[phase]], hop), device_id_type=MESH,
            )

        def at_axis(p, phase, hop=0):
            return (spot[orders[p][phase]] + hop) % 4

        def scatter_a(p, hop):
            at = pl.ds(p * 16 + at_axis(p, 0, hop) * 4, 4)
            return copy(mid.at[at], in_a.at[p, hop - 1], 0, p, hop)

        def scatter_b(p, hop):
            return copy(mid_b.at[p, at_axis(p, 1, hop)], in_b.at[p, hop - 1], 1, p, hop)

        def swap_c(p, hop, arriving=False):
            to = at_axis(p, 2, -hop if arriving else 0)
            return copy(in_c.at[p, at_axis(p, 2)], in_c.at[p, to], 2, p, hop)

        def spread_b(p, hop, arriving=False):
            to = at_axis(p, 1, -hop if arriving else 0)
            return copy(got_b.at[p, at_axis(p, 1)], got_b.at[p, to], 3, p, hop)

        def spread_a(p, hop, arriving=False):
            row = lambda back: pl.ds(core * half_w + p * 16 + at_axis(p, 0, back) * 4, 4)
            return copy(
                full.at[row(0)], full.at[row(-hop if arriving else 0)], 4, p, hop
            )

        def final(p, arriving=False):
            side = 1 - core if arriving else core
            at = pl.ds(side * half_w + p * 16, 16)
            return pltpu.make_async_remote_copy(
                full.at[at], full.at[at], back_send.at[p], back_recv.at[p],
                device_id=other, device_id_type=MESH,
            )

        hops = (2, 1, 3)
        for p in range(3):
            pair(p).start()
        yield
        for p in range(3):
            pair(p).wait_recv()

            @pl.loop(0, 16)
            def _(n):
                total = acc[p * 16 + n] + peer[p * 16 + n].astype(F32)
                acc[p * 16 + n] = total
                mid[p * 16 + n] = total.astype(BF16)

            for hop in hops:
                scatter_a(p, hop).start()
        yield
        for p in range(3):
            for hop in hops:
                scatter_a(p, hop).wait_recv()

            @pl.loop(0, 4)
            def _(n):
                at = p * 16 + at_axis(p, 0) * 4 + n
                total = acc[at]
                for i in range(3):
                    total = total + in_a[p, i, n].astype(F32)
                acc[at] = total
                mid_b[p, n] = total.astype(BF16)

            for hop in hops:
                scatter_b(p, hop).start()
        yield
        for p in range(3):
            for hop in hops:
                scatter_b(p, hop).wait_recv()
            total = acc[p * 16 + at_axis(p, 0) * 4 + at_axis(p, 1)]
            for i in range(3):
                total = total + in_b[p, i].astype(F32)
            in_c[p, at_axis(p, 2)] = total.astype(BF16)
            for hop in hops:
                swap_c(p, hop).start()
        yield
        for p in range(3):
            for hop in hops:
                swap_c(p, hop, True).wait_recv()
            total = in_c[p, 0].astype(F32)
            for i in range(1, 4):
                total = total + in_c[p, i].astype(F32)
            got_b[p, at_axis(p, 1)] = total.astype(BF16)
            for hop in hops:
                spread_b(p, hop).start()
        yield
        for p in range(3):
            for hop in hops:
                spread_b(p, hop, True).wait_recv()

            @pl.loop(0, 4)
            def _(n):
                full[core * half_w + p * 16 + at_axis(p, 0) * 4 + n] = got_b[p, n]

            for hop in hops:
                spread_a(p, hop).start()
        yield
        for p in range(3):
            for hop in hops:
                spread_a(p, hop, True).wait_recv()
            final(p).start()
        yield
        for p in range(3):
            final(p, True).wait_recv()
        done = pltpu.make_async_copy(full, out_ref, out_sem)
        done.start()
        yield
        for p in range(3):
            pair(p).wait_send()
            final(p).wait_send()
            for hop in hops:
                scatter_a(p, hop).wait_send()
                scatter_b(p, hop).wait_send()
                swap_c(p, hop).wait_send()
                spread_b(p, hop).wait_send()
                spread_a(p, hop).wait_send()
        done.wait()

    def kernel(part_in, a, b, c, d, out_ref, weights_ref, part_ref, part_sem, *scratch):
        weights = reduce_steps(
            (a, b, c, d), scratch[:4], scratch[4], weights_ref, *scratch[16:]
        )
        blocks_back = collect_steps(part_in, part_ref, part_sem, out_ref, *scratch[5:16])
        for step in "wbwwbwbbwbwwwbwbw":
            next(weights if step == "w" else blocks_back, None)

    shape = lambda *s: pltpu.VMEM(s + (rows, width), partial.dtype)
    bf = lambda *s: pltpu.VMEM(s + (block, width), BF16)
    dma = lambda *s: pltpu.SemaphoreType.DMA(s)
    vmem = pl.BlockSpec(memory_space=pltpu.VMEM)
    past_grad, weights = pl.pallas_call(
        kernel,
        out_shape=(
            jax.ShapeDtypeStruct((blocks, rows, width), partial.dtype),
            jax.ShapeDtypeStruct((2 * half_w, block, width), BF16),
        ),
        in_specs=[pl.BlockSpec(memory_space=pl.ANY)] * 5,
        out_specs=(vmem, pl.BlockSpec(memory_space=pl.ANY)),
        scratch_shapes=[
            shape(groups, blocks), pltpu.SemaphoreType.DMA,
            *[pltpu.VMEM(a.shape, a.dtype) for a in grads], dma(4),
            shape(2, blocks), shape(2, blocks), shape(2, 2, blocks), shape(blocks), shape(blocks),
            dma(2, 4), dma(2, 4), dma(2, 4, 2), dma(2, 4, 2), dma(4), dma(4),
            pltpu.VMEM((half_w, block, width), F32),
            bf(half_w), bf(half_w), bf(half_w), bf(3, 3, 4), bf(3, 4), bf(3, 3), bf(3, 4), bf(3, 4),
            bf(2 * half_w),
            dma(3), dma(3), dma(5, 3, 3), dma(5, 3, 3), dma(3), dma(3), pltpu.SemaphoreType.DMA,
        ],
        compiler_params=pltpu.CompilerParams(
            collective_id=2, has_side_effects=True, vmem_limit_bytes=62 << 20
        ),
        name="collect",
    )(partial, *grads)
    return past_grad, weights.reshape(4, w_rows, width)


def scatter_sum(source, target, used, outputs):
    count, rows, width = source.shape
    step = 8

    def kernel(target_ref, used_ref, source_ref, out_ref, acc):
        t = pl.program_id(0)

        @pl.when(t == 0)
        def _():
            acc[...] = jnp.zeros_like(acc)

        for j in range(step):
            @pl.when(used_ref[t * step + j] > 0)
            def _():
                m = target_ref[t * step + j]
                acc[m] = acc[m] + source_ref[j].astype(F32)

        @pl.when(t == pl.num_programs(0) - 1)
        def _():
            out_ref[...] = acc[...].astype(out_ref.dtype)

    return pl.pallas_call(
        kernel,
        out_shape=jax.ShapeDtypeStruct((outputs, rows, width), source.dtype),
        grid_spec=pltpu.PrefetchScalarGridSpec(
            num_scalar_prefetch=2,
            grid=(count // step,),
            in_specs=[pl.BlockSpec((step, rows, width), lambda t, *_: (t, 0, 0))],
            out_specs=pl.BlockSpec((outputs, rows, width), lambda t, *_: (0, 0, 0)),
            scratch_shapes=[pltpu.VMEM((outputs, rows, width), F32)],
        ),
        compiler_params=pltpu.CompilerParams(vmem_limit_bytes=48 << 20),
        name="scatter_sum",
    )(target, used, source)


def layer(position, live, arrived, tokens, grad_out, w_query, w_pair, w_out, slots):
    patches, block, width = tokens.shape
    requests = position.shape[0] // patches
    far = requests * block
    rows = block + far
    chunks = 1
    chunk = far // chunks
    pairs = width // 128
    parts = requests + 1

    def kernel(
        position_ref, live_ref, arrived_ref, tokens_ref, grad_ref, wq_ref, wkv_ref, wo_ref,
        attn_ref, tokgrad_ref, fargrad_ref, x_ref, dkv_ref, dq_ref, mixed_ref,
        key_s, val_s, q_s, up_s, s_s, dp_s, pb_s, ds_s, fg_s, in_sem, out_sem,
    ):
        p = pl.program_id(0)

        def fetch(r):
            return pltpu.make_async_copy(
                arrived_ref.at[position_ref[p * requests + r]],
                x_ref.at[0, pl.ds(block + r * block, block)],
                in_sem.at[r],
            )

        for r in range(requests):
            fetch(r).start()
        tok = tokens_ref[0]
        x_ref[0, 0:block] = tok
        q_s[...] = mm(tok, wq_ref[...]).astype(BF16)
        own = mm(tok, wkv_ref[...]).astype(BF16)
        key_s[0:block] = own[:, :width]
        val_s[0:block] = own[:, width:]
        up_s[...] = mm(grad_ref[0], wo_ref[...], NT).astype(BF16)
        for r in range(requests):
            fetch(r).wait()

        @pl.loop(0, chunks)
        def _(c):
            at = pl.multiple_of(block + c * chunk, 128)
            x = x_ref[0, pl.ds(at, chunk)]
            key_s[pl.ds(at, chunk)] = mm(x, wkv_ref[:, :width]).astype(BF16)
            val_s[pl.ds(at, chunk)] = mm(x, wkv_ref[:, width:]).astype(BF16)

        low = lax.broadcasted_iota(jnp.int32, (block, 128), 1) < HD
        zero = jnp.zeros((block, 128), BF16)

        @pl.loop(0, pairs)
        def _(j):
            lanes = pl.ds(pl.multiple_of(j * 128, 128), 128)
            k = key_s[:, lanes]
            v = val_s[:, lanes]
            q = q_s[:, lanes] * jnp.asarray(1.0 / math.sqrt(HD), BF16)
            u = up_s[:, lanes]
            q2 = jnp.concatenate([jnp.where(low, q, zero), jnp.where(low, zero, q)], axis=0)
            u2 = jnp.concatenate([jnp.where(low, u, zero), jnp.where(low, zero, u)], axis=0)
            s_s[...] = mm(k, q2, NT)
            dp_s[...] = mm(v, u2, NT)

            def bias(r):
                dead = live_ref[p * requests + jnp.maximum(r - 1, 0)] == 0
                return jnp.where((r > 0) & dead, -jnp.inf, 0.0).astype(F32)

            def part(r):
                return pl.ds(pl.multiple_of(r * block, block), block)

            def largest(r, m):
                s = s_s[part(r)] + bias(r)
                return jnp.maximum(m, jnp.max(s.reshape(block // 8, 8, 2 * block), axis=0))

            m = lax.fori_loop(0, parts, largest, jnp.full((8, 2 * block), -jnp.inf, F32), unroll=True)
            m = jnp.max(m, axis=0, keepdims=True)

            def exps(r, carry):
                total, delta = carry
                e = jnp.exp(s_s[part(r)] + bias(r) - m)
                s_s[part(r)] = e
                g = e * dp_s[part(r)]
                fold = lambda t: jnp.sum(t.reshape(block // 8, 8, 2 * block), axis=0)
                return total + fold(e), delta + fold(g)

            nil = jnp.zeros((8, 2 * block), F32)
            total, delta = lax.fori_loop(0, parts, exps, (nil, nil), unroll=True)
            inverse = 1.0 / jnp.sum(total, axis=0, keepdims=True)
            delta = jnp.sum(delta, axis=0, keepdims=True) * inverse

            @pl.loop(0, parts, unroll=True)
            def _(r):
                prob = s_s[part(r)] * inverse
                pb_s[part(r)] = prob.astype(BF16)
                ds_s[part(r)] = (prob * (dp_s[part(r)] - delta)).astype(BF16)

            pb = pb_s[...]
            ds = ds_s[...]
            dkv_ref[0, :, lanes] = mm(ds, q2).astype(BF16)
            dkv_ref[0, :, pl.ds(pl.multiple_of(width + j * 128, 128), 128)] = mm(pb, u2).astype(BF16)
            o = mm(pb, v, TN)
            mixed_ref[0, :, lanes] = jnp.where(low, o[:block], o[block:]).astype(BF16)
            dq = mm(ds, k, TN)
            dq = jnp.where(low, dq[:block], dq[block:]) * (1.0 / math.sqrt(HD))
            dq_ref[0, :, lanes] = dq.astype(BF16)

        attn_ref[0] = mm(mixed_ref[0], wo_ref[...]).astype(BF16)
        tokgrad_ref[0] = (
            mm(dq_ref[0], wq_ref[...], NT) + mm(dkv_ref[0, 0:block], wkv_ref[...], NT)
        ).astype(BF16)

        @pl.loop(0, chunks)
        def _(c):
            at = pl.multiple_of(block + c * chunk, 128)
            g = mm(dkv_ref[0, pl.ds(at, chunk)], wkv_ref[...], NT).astype(BF16)
            fg_s[pl.ds(pl.multiple_of(c * chunk, 128), chunk)] = g

        def put(r):
            return pltpu.make_async_copy(
                fg_s.at[pl.ds(r * block, block)],
                fargrad_ref.at[position_ref[p * requests + r]],
                out_sem.at[r],
            )

        for r in range(requests):
            @pl.when(live_ref[p * requests + r] > 0)
            def _():
                put(r).start()

        for r in range(requests):
            @pl.when(live_ref[p * requests + r] > 0)
            def _():
                put(r).wait()

    per_patch = lambda n, w: pl.BlockSpec((1, n, w), lambda p, *_: (p, 0, 0))
    whole = lambda a: pl.BlockSpec(a.shape, lambda p, *_: (0, 0), pipeline_mode=pl.Buffered(1))
    hbm = pl.BlockSpec(memory_space=pl.ANY)
    shape = lambda *s: jax.ShapeDtypeStruct(s, BF16)
    return pl.pallas_call(
        kernel,
        out_shape=(
            shape(patches, block, width),
            shape(patches, block, width),
            shape(slots, block, width),
            shape(patches, rows, width),
            shape(patches, rows, 2 * width),
            shape(patches, block, width),
            shape(patches, block, width),
        ),
        grid_spec=pltpu.PrefetchScalarGridSpec(
            num_scalar_prefetch=2,
            grid=(patches,),
            in_specs=[
                hbm, per_patch(block, width), per_patch(block, width),
                whole(w_query), whole(w_pair), whole(w_out),
            ],
            out_specs=(
                per_patch(block, width), per_patch(block, width), hbm, per_patch(rows, width),
                per_patch(rows, 2 * width), per_patch(block, width), per_patch(block, width),
            ),
            scratch_shapes=[
                pltpu.VMEM((rows, width), BF16),
                pltpu.VMEM((rows, width), BF16),
                pltpu.VMEM((block, width), BF16),
                pltpu.VMEM((block, width), BF16),
                pltpu.VMEM((rows, 2 * block), F32),
                pltpu.VMEM((rows, 2 * block), F32),
                pltpu.VMEM((rows, 2 * block), BF16),
                pltpu.VMEM((rows, 2 * block), BF16),
                pltpu.VMEM((far, width), BF16),
                pltpu.SemaphoreType.DMA((requests,)),
                pltpu.SemaphoreType.DMA((requests,)),
            ],
        ),
        compiler_params=pltpu.CompilerParams(vmem_limit_bytes=60 << 20),
        name="layer",
    )(position, live, arrived, tokens, grad_out, w_query, w_pair, w_out)


def body(
    query_tokens, past_tokens, source_dev, source_slot, kept, w_query, w_key, w_value, w_out,
    grad_out,
):
    _, patches, block, width = query_tokens.shape
    tokens, grads, past = query_tokens[0], grad_out[0], past_tokens[0]
    peers = lax.axis_size("patch")
    y, x, z, _ = place()
    per_device = patches * source_dev.shape[1] * source_dev.shape[2]
    blocks = past.shape[0]

    grid = lambda a: a.reshape(4, 2, 4, per_device)
    near = lambda a: jnp.concatenate([grid(a)[y, x], grid(a)[:, x, z]], axis=0)
    owner, slot, kept = (a.reshape(peers, per_device) for a in (source_dev, source_slot, kept))
    from_y, half, from_z = owner // 8, (owner // 4) % 2, owner % 4
    key = half * 4 + jnp.where(half == 0, from_z, from_y)
    number = jnp.where(half == 0, from_y, from_z) * blocks + slot
    key = jnp.where(kept > 0, key, 8)
    most = jnp.max(jnp.sum((key[:, None, :] == jnp.arange(8)[None, :, None]).astype(jnp.int32), axis=2))
    key, number = near(key), near(number)
    order = jnp.arange(per_device)
    matches = (key[:, :, None] == key[:, None, :]) & (order[:, None] > order[None, :])
    rank = jnp.sum(matches.astype(jnp.int32), axis=2)
    chosen_here = jnp.where(jnp.arange(8) < 4, z, 4 + y)
    live = grid(kept)[y, x, z]
    w_pair = jnp.concatenate([w_key, w_value], axis=1)
    flat = lambda a: a.reshape(-1, a.shape[-1])

    few, many = 6, 8
    small = most <= few
    cap = jnp.where(small, few, many)

    def pick(a):
        tight = jnp.pad(a[:, :few].reshape(-1), (0, 8 * (many - few)))
        return jnp.where(small, tight, a.reshape(-1))

    hit = (rank[:, :, None] == jnp.arange(many)) & (key == chosen_here[:, None])[:, :, None]
    table = jnp.sum(jnp.where(hit, number[:, :, None], 0), axis=1)
    used = pick(jnp.sum(hit.astype(jnp.int32), axis=1))
    target = pick(table + jnp.where(jnp.arange(8) < 4, 0, 4 * blocks)[:, None])
    table = pick(table)
    mine = jnp.where(live > 0, key[z] * cap + rank[z], 0)
    arrived = lax.cond(
        small, lambda: spread(past, table, few, 0), lambda: spread(past, table, many, 3)
    )
    attn, token_grad, far_grad, seen, dkv, dq, mixed = layer(
        mine, live, arrived, tokens, grads, w_query, w_pair, w_out, 8 * many
    )
    back = (far_grad, flat(tokens), flat(grads), flat(seen), flat(dkv), flat(dq), flat(mixed))
    returned, *weight_grads = lax.cond(
        small, lambda: send_back(*back, few, 1), lambda: send_back(*back, many, 4)
    )
    partial = scatter_sum(returned, target, used, 8 * blocks)
    scale = 1.0 / math.sqrt(lax.axis_size("dp") * peers * patches * block)
    past_grad, weights = collect(partial.reshape((8,) + past.shape), weight_grads, scale)
    weights = weights.astype(F32)
    return (
        attn[None],
        token_grad[None],
        past_grad[None],
        weights[0],
        weights[1],
        weights[2],
        weights[3],
    )


def solution(mesh):
    split = P("dp", "patch", None, None)
    return jax.shard_map(
        body,
        mesh=mesh,
        in_specs=(split, split, P(), P(), P(), P(), P(), P(), P(), split),
        out_specs=(split, split, split, P(), P(), P(), P()),
        check_vma=False,
    )
```

profile of v0, /device:TPU:1, one launch (start us, length us, event | category | flops | bytes accessed | tf_op | source)
XLA Modules:
  0.0 382.8 jit_solution(4850501886595586590)
XLA Ops:
  0.7 0.7 broadcast_compare_fusion.2
  1.5 0.1 add.129
  1.6 0.1 copy.24
  1.7 0.1 gt.36
  1.8 0.8 copy.23
  2.7 0.1 reshape.214
  2.8 0.1 reshape.213
  3.1 0.6 reduce_max.9
  4.4 0.8 copy.27
  5.2 0.1 reshape.215
  5.3 0.8 copy.22
  6.2 0.1 reshape_reshape.3
  6.3 0.1 multiply_add_fusion
  6.4 0.1 broadcast_compare_fusion.3
  6.5 0.3 convert_reduce_fusion
  6.8 0.5 compare_select_fusion
  7.3 0.3 convert_reduce_fusion.2
  7.7 0.1 reshape.216
  7.8 0.1 reshape.219
  7.9 0.1 reshape.220
  8.0 0.1 reshape.217
  8.1 0.1 reshape.218
  8.2 3.2 pad_maximum_fusion.wkv_ref
  11.4 122.1 %conditional.2 = (bf16[64,128,768]{2,1,0:T(8,128)(2,1)}) conditional(s32[]{:T(128)} %convert_element_type.19, (s32[64]{0:T(128)S(1)}, bf16[8,128,768]{2,1,0:T(8,128)(2,1)}) %tuple.44, (s32[64]{0:T(128)S(1)}, bf16[8,128,768]{2,1,0:T(8,128)(2,1)}) %tuple.45), branch_computations={%region_4.5_spmd, %region_5.6_spmd} | conditional | bytes 8 | solution.py:877
  11.4 121.9 %spread.3 = bf16[64,128,768]{2,1,0:T(8,128)(2,1)} custom-call(s32[64]{0:T(128)S(1)} %get-tuple-element.41.table_ref, bf16[8,128,768]{2,1,0:T(8,128)(2,1)} %get-tuple-element.42.past_ref), custom_call_target="tpu_custom_call" | custom-call | tf_op jit(solution)/shard_map/cond/branch_1_fun/spread/pallas_call | solution.py:166
  133.6 64.3 %layer.1 = (bf16[2,128,768]{2,1,0:T(8,128)(2,1)}, bf16[2,128,768]{2,1,0:T(8,128)(2,1)}, bf16[64,128,768]{2,1,0:T(8,128)(2,1)}, bf16[2,1664,768]{2,1,0:T(8,128)(2...) custom-call(s32[24]{0:T(128)} %get-tuple-element.94.position_ref, ...), custom_call_target="tpu_custom_call" | custom-call | tf_op jit(solution)/shard_map/layer/pallas_call | solution.py:794
  197.8 59.3 %conditional.3 = ((bf16[64,128,768]{2,1,0:T(8,128)(2,1)}, f32[768,768]{1,0:T(8,128)}, f32[768,768]{1,0:T(8,128)}, f32[768,768]{1,0:T(8,128)}, f32[768,768]{1,0:T(8,128)})) conditional(s32[]{:T(128)} %convert_element_type.19, (bf16[64,128,768]{2,1,0:T(8,128)(2,1)}, bf16[256,768]{1,0:T(8,128)(2,1)S(1)}, bf16[256,768]{1,0:T(8,128)(2,1)S(1)}, ...), branch_computations={%region_7.8_spmd, %region_8.9_spmd} | conditional | bytes 8 | solution.py:884
  198.1 59.0 %send_back.3 = (bf16[64,128,768]{2,1,0:T(8,128)(2,1)}, f32[768,768]{1,0:T(8,128)}, f32[768,768]{1,0:T(8,128)}, f32[768,768]{1,0:T(8,128)}, f32[768,768]{1,0:T(8,128)}) custom-call(bf16[64,128,768]{2,1,0:T(8,128)(2,1)} %get-tuple-element.50.grad_ref, bf16[256,768]{1,0:T(8,128)(2,1)S(1)} %get-tuple-element.51.tok_in, ...), custom_call_target="tpu_custom_call" | custom-call | tf_op jit(solution)/shard_map/cond/branch_1_fun/send_back/pallas_call | solution.py:262
  257.1 15.0 %scatter_sum.1 = bf16[64,128,768]{2,1,0:T(8,128)(2,1)} custom-call(s32[64]{0:T(128)S(1)} %get-tuple-element.102.target_ref, s32[64]{0:T(128)S(1)} %broadcast_select_fusion.used_ref, bf16[64,128,768]{2,1,0:T(8,128)(2,1)} %get-tuple-element.85.source_ref), custom_call_target="tpu_custom_call" | custom-call | tf_op jit(solution)/shard_map/scatter_sum/pallas_call | solution.py:646
  272.1 102.9 %collect.1 = (bf16[8,128,768]{2,1,0:T(8,128)(2,1)}, bf16[96,32,768]{2,1,0:T(8,128)(2,1)}) custom-call(bf16[8,8,128,768]{3,2,1,0:T(8,128)(2,1)} %bitcast.31, f32[768,768]{1,0:T(8,128)} %get-tuple-element.86.a, f32[768,768]{1,0:T(8,128)} %get-tuple-element.87.b, f32[768,768]{1,0:T(8,128)} %get-tuple-element.88.c, f32[768,768]{1,0:T(8,128)} %get-tuple-element.89.d), custom_call_target="tpu_custom_call" | custom-call | tf_op jit(solution)/shard_map/collect/pallas_call | solution.py:599
  375.0 6.6 %fusion.16 = (f32[24,32,768]{2,1,0:T(8,128)}, f32[24,32,768]{2,1,0:T(8,128)}, f32[24,32,768]{2,1,0:T(8,128)}, f32[24,32,768]{2,1,0:T(8,128)}) fusion(bf16[96,32,768]{2,1,0:T(8,128)(2,1)} %get-tuple-element.91), kind=kLoop, calls=%fused_computation.69 | loop fusion | bytes 18874368 | tf_op jit(solution)/shard_map/slice | solution.py:898
  381.6 1.1 copy.41
  (20 shorter events, 0.4 us)
Async XLA Ops:
  11.4 122.1 %copy-start = (bf16[1,2,128,768]{3,2,1,0:T(8,128)(2,1)S(1)}, bf16[1,2,128,768]{3,2,1,0:T(8,128)(2,1)}, u32[]{:S(2)}) copy-start(bf16[1,2,128,768]{3,2,1,0:T(8,128)(2,1)} %param.14) | copy-start | bytes 1179652
  11.4 122.1 %copy-start.1 = (bf16[1,2,128,768]{3,2,1,0:T(8,128)(2,1)S(1)}, bf16[1,2,128,768]{3,2,1,0:T(8,128)(2,1)}, u32[]{:S(2)}) copy-start(bf16[1,2,128,768]{3,2,1,0:T(8,128)(2,1)} %param.23) | copy-start | bytes 1179652
  375.0 6.6 %copy-start.2 = (bf16[8,128,768]{2,1,0:T(8,128)(2,1)S(1)}, bf16[8,128,768]{2,1,0:T(8,128)(2,1)}, u32[]{:S(2)}) copy-start(bf16[8,128,768]{2,1,0:T(8,128)(2,1)} %get-tuple-element.90) | copy-start | bytes 4718596
where the time goes:
time: 383 us
  Pallas kernels  363 us (95%)
  local copies, waits for them, and re-layouts  11.7 us (3%)
  other arithmetic  6.03 us (2%)
    pallas_call x1, Pallas kernels, spread(): pl.pallas_call(kernel, out_shape=jax.ShapeDtypeStruct((table.shape[0], ro...  122 us
    pallas_call x1, Pallas kernels, collect(): pl.pallas_call(kernel, out_shape=(jax.ShapeDtypeStruct((blocks, rows, wid...  103 us
    pallas_call x1, Pallas kernels, layer(): pl.pallas_call(kernel, out_shape=(shape(patches, block, width), shape(pat...  64.3 us
    pallas_call x1, Pallas kernels, send_back(): pl.pallas_call(kernel, out_shape=(jax.ShapeDtypeStruct(grads.shape, grads...  59 us
    pallas_call x1, Pallas kernels, scatter_sum(): pl.pallas_call(kernel, out_shape=jax.ShapeDtypeStruct((outputs, rows, wid...  15 us

commit v1 on v0

--- a/solution.py
+++ b/solution.py
@@ -615,7 +615,7 @@
             dma(3), dma(3), dma(5, 3, 3), dma(5, 3, 3), dma(3), dma(3), pltpu.SemaphoreType.DMA,
         ],
         compiler_params=pltpu.CompilerParams(
-            collective_id=2, has_side_effects=True, vmem_limit_bytes=62 << 20
+            collective_id=6, has_side_effects=True, vmem_limit_bytes=62 << 20
         ),
         name="collect",
     )(partial, *grads)
@@ -860,13 +860,16 @@
     w_pair = jnp.concatenate([w_key, w_value], axis=1)
     flat = lambda a: a.reshape(-1, a.shape[-1])
 
-    few, many = 6, 8
-    small = most <= few
-    cap = jnp.where(small, few, many)
+    caps = (5, 6, 8)
+    many = caps[-1]
+    size = (most > caps[0]).astype(jnp.int32) + (most > caps[1]).astype(jnp.int32)
+    by_size = lambda options: jnp.where(
+        size == 0, options[0], jnp.where(size == 1, options[1], options[2])
+    )
+    cap = by_size(caps)
 
     def pick(a):
-        tight = jnp.pad(a[:, :few].reshape(-1), (0, 8 * (many - few)))
-        return jnp.where(small, tight, a.reshape(-1))
+        return by_size([jnp.pad(a[:, :n].reshape(-1), (0, 8 * (many - n))) for n in caps])
 
     hit = (rank[:, :, None] == jnp.arange(many)) & (key == chosen_here[:, None])[:, :, None]
     table = jnp.sum(jnp.where(hit, number[:, :, None], 0), axis=1)
@@ -874,15 +877,15 @@
     target = pick(table + jnp.where(jnp.arange(8) < 4, 0, 4 * blocks)[:, None])
     table = pick(table)
     mine = jnp.where(live > 0, key[z] * cap + rank[z], 0)
-    arrived = lax.cond(
-        small, lambda: spread(past, table, few, 0), lambda: spread(past, table, many, 3)
+    arrived = lax.switch(
+        size, [lambda n=n, i=i: spread(past, table, n, 2 * i) for i, n in enumerate(caps)]
     )
     attn, token_grad, far_grad, seen, dkv, dq, mixed = layer(
         mine, live, arrived, tokens, grads, w_query, w_pair, w_out, 8 * many
     )
     back = (far_grad, flat(tokens), flat(grads), flat(seen), flat(dkv), flat(dq), flat(mixed))
-    returned, *weight_grads = lax.cond(
-        small, lambda: send_back(*back, few, 1), lambda: send_back(*back, many, 4)
+    returned, *weight_grads = lax.switch(
+        size, [lambda n=n, i=i: send_back(*back, n, 2 * i + 1) for i, n in enumerate(caps)]
     )
     partial = scatter_sum(returned, target, used, 8 * blocks)
     scale = 1.0 / math.sqrt(lax.axis_size("dp") * peers * patches * block)

time: 383 us -> 367 us (0.958)
  Pallas kernels: 363 us -> 346 us
    pallas_call x1, Pallas kernels: 59 us -> 50.3 us  [send_back(): pl.pallas_call(kernel, out_shape=(jax.ShapeDtypeStruct(grads.shape, grads...]
    pallas_call x1, Pallas kernels: 122 us -> 113 us  [spread(): pl.pallas_call(kernel, out_shape=jax.ShapeDtypeStruct((table.shape[0], ro...]
where the time goes in v1:
time: 367 us; the launch traced here: 366 us
  Pallas kernels  346 us (94%)
  local copies, waits for them, and re-layouts  11.9 us (3%)
  other arithmetic  5.76 us (2%)
    pallas_call x1, Pallas kernels, spread(): pl.pallas_call(kernel, out_shape=jax.ShapeDtypeStruct((table.shape[0], ro...  113 us
    pallas_call x1, Pallas kernels, collect(): pl.pallas_call(kernel, out_shape=(jax.ShapeDtypeStruct((blocks, rows, wid...  103 us
    pallas_call x1, Pallas kernels, layer(): pl.pallas_call(kernel, out_shape=(shape(patches, block, width), shape(pat...  64.3 us
    pallas_call x1, Pallas kernels, send_back(): pl.pallas_call(kernel, out_shape=(jax.ShapeDtypeStruct(grads.shape, grads...  50.3 us
    pallas_call x1, Pallas kernels, scatter_sum(): pl.pallas_call(kernel, out_shape=jax.ShapeDtypeStruct((outputs, rows, wid...  14.8 us

profile of v1, /device:TPU:1, one launch (start us, length us, event | category | flops | bytes accessed | tf_op | source)
XLA Modules:
  0.0 366.2 jit_solution(17968651142941855591)
XLA Ops:
  0.7 0.8 broadcast_compare_fusion.2
  1.6 0.1 add.139
  1.7 0.1 copy.24
  1.8 0.1 gt.42
  1.9 0.8 copy.23
  2.8 0.1 reshape.223
  2.9 0.1 reshape.222
  3.2 0.6 reduce_max.9
  5.1 0.8 copy.27
  5.9 0.1 reshape.224
  6.1 0.8 copy.22
  6.9 0.1 reshape_reshape.3
  7.3 0.3 convert_reduce_fusion
  7.6 0.5 compare_select_fusion
  8.1 0.3 convert_reduce_fusion.2
  8.4 0.1 reshape.225
  8.5 0.1 reshape.226
  8.6 0.1 reshape.230
  8.7 0.1 reshape.231
  8.8 0.1 reshape.232
  9.0 0.1 reshape.228
  9.1 0.1 reshape.229
  9.2 2.9 pad_maximum_fusion.wkv_ref
  12.1 113.6 %conditional.2 = (bf16[64,128,768]{2,1,0:T(8,128)(2,1)}) conditional(s32[]{:T(128)} %clamp.4, (s32[64]{0:T(128)S(1)}, bf16[8,128,768]{2,1,0:T(8,128)(2,1)}) %tuple.55, (s32[64]{0:T(128)S(1)}, bf16[8,128,768]{2,1,0:T(8,128)(2,1)}) %tuple.56, (s32[64]{0:T(128)S(1)}, bf16[8,128,768]{2,1,0:T(8,128)(2,1)}) %tuple.57), branch_computations={%region_4.5_spmd, %region_5.6_spmd, %region_6.7_spmd} | conditional | bytes 8 | solution.py:880
  12.1 113.4 %spread.3 = bf16[64,128,768]{2,1,0:T(8,128)(2,1)} custom-call(s32[64]{0:T(128)S(1)} %get-tuple-element.32.table_ref, bf16[8,128,768]{2,1,0:T(8,128)(2,1)} %get-tuple-element.46.past_ref), custom_call_target="tpu_custom_call" | custom-call | tf_op jit(solution)/shard_map/cond/branch_0_fun/spread/pallas_call | solution.py:166
  125.7 64.3 %layer.1 = (bf16[2,128,768]{2,1,0:T(8,128)(2,1)}, bf16[2,128,768]{2,1,0:T(8,128)(2,1)}, bf16[64,128,768]{2,1,0:T(8,128)(2,1)}, bf16[2,1664,768]{2,1,0:T(8,128)(2...) custom-call(s32[24]{0:T(128)} %get-tuple-element.122.position_ref, ...), custom_call_target="tpu_custom_call" | custom-call | tf_op jit(solution)/shard_map/layer/pallas_call | solution.py:794
  190.0 50.5 %conditional.3 = ((bf16[64,128,768]{2,1,0:T(8,128)(2,1)}, f32[768,768]{1,0:T(8,128)}, f32[768,768]{1,0:T(8,128)}, f32[768,768]{1,0:T(8,128)}, f32[768,768]{1,0:T(8,128)})) conditional(s32[]{:T(128)} %clamp.4, (bf16[64,128,768]{2,1,0:T(8,128)(2,1)}, bf16[256,768]{1,0:T(8,128)(2,1)S(1)}, bf16[256,768]{1,0:T(8,128)(2,1)S(1)}, ...), branch_computations={%region_8.9_spmd, %region_9.10_spmd, %region_10.11_spmd} | conditional | bytes 8 | solution.py:887
  190.2 50.3 %send_back.3 = (bf16[64,128,768]{2,1,0:T(8,128)(2,1)}, f32[768,768]{1,0:T(8,128)}, f32[768,768]{1,0:T(8,128)}, f32[768,768]{1,0:T(8,128)}, f32[768,768]{1,0:T(8,128)}) custom-call(bf16[64,128,768]{2,1,0:T(8,128)(2,1)} %get-tuple-element.64.grad_ref, bf16[256,768]{1,0:T(8,128)(2,1)S(1)} %get-tuple-element.65.tok_in, ...), custom_call_target="tpu_custom_call" | custom-call | tf_op jit(solution)/shard_map/cond/branch_0_fun/send_back/pallas_call | solution.py:262
  240.5 14.8 %scatter_sum.1 = bf16[64,128,768]{2,1,0:T(8,128)(2,1)} custom-call(s32[64]{0:T(128)S(1)} %get-tuple-element.130.target_ref, s32[64]{0:T(128)S(1)} %broadcast_select_fusion.3.used_ref, bf16[64,128,768]{2,1,0:T(8,128)(2,1)} %get-tuple-element.113.source_ref), custom_call_target="tpu_custom_call" | custom-call | tf_op jit(solution)/shard_map/scatter_sum/pallas_call | solution.py:646
  255.3 103.1 %collect.1 = (bf16[8,128,768]{2,1,0:T(8,128)(2,1)}, bf16[96,32,768]{2,1,0:T(8,128)(2,1)}) custom-call(bf16[8,8,128,768]{3,2,1,0:T(8,128)(2,1)} %bitcast.37, f32[768,768]{1,0:T(8,128)} %get-tuple-element.114.a, f32[768,768]{1,0:T(8,128)} %get-tuple-element.115.b, f32[768,768]{1,0:T(8,128)} %get-tuple-element.116.c, f32[768,768]{1,0:T(8,128)} %get-tuple-element.117.d), custom_call_target="tpu_custom_call" | custom-call | tf_op jit(solution)/shard_map/collect/pallas_call | solution.py:599
  358.4 6.6 %fusion.16 = (f32[24,32,768]{2,1,0:T(8,128)}, f32[24,32,768]{2,1,0:T(8,128)}, f32[24,32,768]{2,1,0:T(8,128)}, f32[24,32,768]{2,1,0:T(8,128)}) fusion(bf16[96,32,768]{2,1,0:T(8,128)(2,1)} %get-tuple-element.119), kind=kLoop, calls=%fused_computation.72 | loop fusion | bytes 18874368 | tf_op jit(solution)/shard_map/slice | solution.py:901
  365.0 1.1 copy.47
  (25 shorter events, 0.6 us)
Async XLA Ops:
  0.6 8.6 %copy-start.3 = (bf16[768,768]{1,0:T(8,128)(2,1)S(1)}, bf16[768,768]{1,0:T(8,128)(2,1)}, u32[]{:S(2)}) copy-start(bf16[768,768]{1,0:T(8,128)(2,1)} %param.23) | copy-start | bytes 3538948
  12.1 113.6 %copy-start = (bf16[1,2,128,768]{3,2,1,0:T(8,128)(2,1)S(1)}, bf16[1,2,128,768]{3,2,1,0:T(8,128)(2,1)}, u32[]{:S(2)}) copy-start(bf16[1,2,128,768]{3,2,1,0:T(8,128)(2,1)} %param.16) | copy-start | bytes 1179652
  12.1 113.6 %copy-start.1 = (bf16[1,2,128,768]{3,2,1,0:T(8,128)(2,1)S(1)}, bf16[1,2,128,768]{3,2,1,0:T(8,128)(2,1)}, u32[]{:S(2)}) copy-start(bf16[1,2,128,768]{3,2,1,0:T(8,128)(2,1)} %param.25) | copy-start | bytes 1179652
  358.4 6.6 %copy-start.2 = (bf16[8,128,768]{2,1,0:T(8,128)(2,1)S(1)}, bf16[8,128,768]{2,1,0:T(8,128)(2,1)}, u32[]{:S(2)}) copy-start(bf16[8,128,768]{2,1,0:T(8,128)(2,1)} %get-tuple-element.118) | copy-start | bytes 4718596
